TPU v7x, 256 devices: a whole 4x4x8 slice. The times are simulated.
256 devices in a mesh: seg: 8 (over x, y_hi), gx: 2 (over y_lo), gz: 16 (over z, core).
Axes of the slice: x: 4, y: 4 (y_hi: 2, y_lo: 2; y = y_hi * 2 + y_lo), z: 8, core: 2. Of those that a mesh axis runs over, the one named last changes fastest.
Arguments:
- terminal: float32 [8, 3, 128, 256, 256], P('seg', None, 'gx', 'gz'), may hold values from -6 to 6
- jump: float32 [8, 3, 128, 256, 256], P('seg', None, 'gx', 'gz'), may hold values from -61 to 61
- tangent: float32 [8, 3, 128, 256, 256], P('seg', None, 'gx', 'gz'), may hold values from -36 to 36
- base_velocity: float32 [256], replicated, may hold values from 0.5 to 2
- base_shear: float32 [256], replicated, may hold values from -2 to 2
Outputs:
- adjoint_field: float32 [8, 3, 128, 256, 256], P('seg', None, 'gx', 'gz')
All inputs are finite; a program needn't handle non-finite values. Where the computation divides by a largest or mean magnitude, that divisor is 1e-20 or more.
Results may differ from a plain program's by a relative error of at most 0.00018.
Values sent between devices are 32-bit elements; how exact they have to be, the bound alone decides.
A program may use at most 64 MiB of HBM per device.

v0:
```python
import jax
import jax.numpy as jnp
import numpy as np
from jax import lax
from jax.sharding import PartitionSpec as P

STEPS = 4


TIME_STEP = 0.15
DIFFUSE = 0.1
WALL_COEF = 0.0002
EPSILON = 1e-06
NEWTON_TURNS = 100


def with_halo(cells, sides, width):
    for axis, dim in sides:
        count = lax.axis_size(axis)
        head = lax.slice_in_dim(cells, 0, width, axis=dim)
        tail = lax.slice_in_dim(cells, cells.shape[dim] - width, cells.shape[dim], axis=dim)
        cells = jnp.concatenate(
            [
                lax.ppermute(tail, axis, [(i, (i + 1) % count) for i in range(count)]),
                cells,
                lax.ppermute(head, axis, [((i + 1) % count, i) for i in range(count)]),
            ],
            axis=dim,
        )
    return cells


def from_behind(value, axis, steps):
    count = lax.axis_size(axis)
    pairs = [(source, (source + steps) % count) for source in range(count)]
    return lax.ppermute(value, axis, pairs)


def invert_newton(matrix):
    order = matrix.shape[0]
    identity = np.eye(order)
    scale_one = np.max(np.sum(np.abs(matrix), axis=0))
    scale_inf = np.max(np.sum(np.abs(matrix), axis=1))
    approx = matrix.T / (scale_one * scale_inf)
    for turn_index in range(NEWTON_TURNS):
        approx = approx @ (2.0 * identity - matrix @ approx)
    return approx


def wall_table(points):
    intervals = points - 1
    cheb_nodes = np.cos(np.pi * np.arange(points) / intervals)
    weights = np.ones(points)
    weights[0] = 2.0
    weights[-1] = 2.0
    weights = weights * (-1.0) ** np.arange(points)
    spread = cheb_nodes[:, None] - cheb_nodes[None, :]
    first_deriv = weights[:, None] / weights[None, :] / (spread + np.eye(points))
    first_deriv = first_deriv - np.eye(points) * first_deriv.sum(axis=1)[:, None]
    second = first_deriv @ first_deriv
    interior = np.eye(points - 2) - WALL_COEF * second[1:-1, 1:-1]
    helm_table = np.zeros((points, points))
    helm_table[1:-1, 1:-1] = invert_newton(interior)
    return jnp.asarray(helm_table.T, dtype=jnp.float32)


def advance(padded, velocity, shear, table_t):
    center = padded[:, 2:-2, 2:-2, :]
    fwd2_x = padded[:, 4:, 2:-2, :]
    fwd1_x = padded[:, 3:-1, 2:-2, :]
    back1_x = padded[:, 1:-3, 2:-2, :]
    back2_x = padded[:, :-4, 2:-2, :]
    fwd2_z = padded[:, 2:-2, 4:, :]
    fwd1_z = padded[:, 2:-2, 3:-1, :]
    back1_z = padded[:, 2:-2, 1:-3, :]
    back2_z = padded[:, 2:-2, :-4, :]
    advect = (back2_x - fwd2_x + 8.0 * (fwd1_x - back1_x)) / 12.0
    lap_x = (16.0 * (fwd1_x + back1_x) - (fwd2_x + back2_x) - 30.0 * center) / 12.0
    lap_z = (16.0 * (fwd1_z + back1_z) - (fwd2_z + back2_z) - 30.0 * center) / 12.0
    explicit = center + TIME_STEP * velocity * advect + DIFFUSE * (lap_x + lap_z)
    explicit = jnp.concatenate(
        [explicit[:1], explicit[1:2] - TIME_STEP * shear * center[:1], explicit[2:]], axis=0
    )
    flattened = explicit.reshape(-1, explicit.shape[-1])
    updated = jnp.dot(
        flattened, table_t, precision=lax.Precision.HIGHEST, preferred_element_type=jnp.float32
    )
    return updated.reshape(explicit.shape)


def extend(adjoint, width):
    along_x = with_halo(adjoint, (("gx", 1),), width)
    return with_halo(along_x, (("gz", 2),), width)


def shards(terminal, jump, tangent, base_velocity, base_shear):
    table_t = wall_table(base_velocity.shape[0])
    received = from_behind(terminal, "seg", -1)
    started = received[0] + jump[0]
    direction = tangent[0]
    products = lax.psum(
        (jnp.sum(started * direction), jnp.sum(direction * direction)), ("gx", "gz")
    )
    along_coef = products[0] / (products[1] + EPSILON)
    adjoint = started - along_coef * direction
    for step_index in range(STEPS):
        padded = extend(adjoint, 2)
        adjoint = advance(padded, base_velocity, base_shear, table_t)
    return adjoint[None]


def solution(mesh):
    in_specs = (
        P("seg", None, "gx", "gz", None),
        P("seg", None, "gx", "gz", None),
        P("seg", None, "gx", "gz", None),
        P(),
        P(),
    )
    out_specs = P("seg", None, "gx", "gz", None)
    return jax.shard_map(shards, mesh=mesh, in_specs=in_specs, out_specs=out_specs, check_vma=False)
```

profile of v0, /device:TPU:22, one launch (start us, length us, event | category | flops | bytes accessed | tf_op | source)
XLA Modules:
  0.0 248.8 jit_solution(7663834592041668082)
XLA Ops:
  0.3 73.3 %collective-permute-done = f32[1,3,64,16,256]{4,3,2,1,0:T(8,128)S(1)} collective-permute-done((f32[1,3,64,16,256]{4,3,2,1,0:T(8,128)}, f32[1,3,64,16,256]{4,3,2,1,0:T(8,128)S(1)}, u32[]{:S(2)}, u32[]{:S(2)}) %collective-permute-start) | collective-permute-done | bytes 3145760 | tf_op jit(solution)/shard_map/ppermute | solution.py:36
  73.7 5.4 %fusion.39 = (f32[]{:T(128)}, f32[]{:T(128)}) fusion(f32[1,3,64,16,256]{4,3,2,1,0:T(8,128)} %param.8, f32[1,3,64,16,256]{4,3,2,1,0:T(8,128)S(1)} %collective-permute-done, f32[1,3,64,16,256]{4,3,2,1,0:T(8,128)} %param.7), kind=kLoop, calls=%fused_computation.85 | loop fusion | flops 3932158 | bytes 9437192 | tf_op jit(solution)/shard_map/reduce_sum | solution.py:102
  79.1 58.7 %all-reduce = (f32[]{:T(128)}, f32[]{:T(128)}) all-reduce(f32[]{:T(128)} %get-tuple-element.6, f32[]{:T(128)} %get-tuple-element.5), channel_id=1, replica_groups=mesh['seg'=8,'gx'=2,'gz'=16] {'gx','gz'}, use_global_device_ids=true, to_apply=%region_1.0 | all-reduce | flops 2 | bytes 16 | tf_op jit(solution)/shard_map/psum | solution.py:101
  139.2 4.0 %fusion.40 = f32[3,64,16,256]{3,2,1,0:T(8,128)S(1)} fusion(f32[1,3,64,16,256]{4,3,2,1,0:T(8,128)S(1)} %copy-done, f32[]{:T(128)S(6)} %div.31, f32[1,3,64,16,256]{4,3,2,1,0:T(8,128)} %copy-done.1, f32[1,3,64,16,256]{4,3,2,1,0:T(8,128)} %param.7), kind=kLoop, calls=%fused_computation.86 | loop fusion | flops 2359296 | bytes 12582916 | tf_op jit(solution)/shard_map/sub | solution.py:105
  145.3 2.6 %collective-permute-done.1 = f32[3,2,16,256]{3,2,1,0:T(8,128)S(1)} collective-permute-done((f32[3,2,16,256]{3,2,1,0:T(8,128)S(1)}, f32[3,2,16,256]{3,2,1,0:T(8,128)S(1)}, u32[]{:S(2)}, u32[]{:S(2)}) %collective-permute-start.1) | collective-permute-done | bytes 98336 | tf_op jit(solution)/shard_map/ppermute | solution.py:24
  149.8 5.0 %collective-permute-done.3 = f32[3,68,2,256]{3,2,1,0:T(2,128)S(1)} collective-permute-done((f32[3,68,2,256]{3,2,1,0:T(2,128)S(1)}, f32[3,68,2,256]{3,2,1,0:T(2,128)S(1)}, u32[]{:S(2)}, u32[]{:S(2)}) %collective-permute-start.3) | collective-permute-done | bytes 417824 | tf_op jit(solution)/shard_map/ppermute | solution.py:26
  154.8 3.1 %collective-permute-done.4 = f32[3,68,2,256]{3,2,1,0:T(2,128)S(1)} collective-permute-done((f32[3,68,2,256]{3,2,1,0:T(2,128)S(1)}, f32[3,68,2,256]{3,2,1,0:T(2,128)S(1)}, u32[]{:S(2)}, u32[]{:S(2)}) %collective-permute-start.4) | collective-permute-done | bytes 417824 | tf_op jit(solution)/shard_map/ppermute | solution.py:24
  158.0 1.3 pad_maximum_fusion
  159.3 4.1 %fusion.30 = f32[3,64,16,256]{3,2,1,0:T(8,128)} fusion(f32[3,68,18,256]{3,2,1,0:T(8,128)S(1)} %get-tuple-element.22, f32[3,68,18,256]{3,2,1,0:T(8,128)S(1)} %get-tuple-element.21, f32[3,64,16,256]{3,2,1,0:T(8,128)S(1)} %fusion.40, f32[3,2,16,256]{3,2,1,0:T(8,128)S(1)} %collective-permute-done.2, f32[3,2,16,256]{3,2,1,0:T(8,128)S(1)} %collective-permute-done.1, ...), kind=kLoop, calls=%fused_computation.67 | loop fusion | flops 18874368 | bytes 19072000 | tf_op jit(solution)/shard_map/add | solution.py:80
  163.4 2.3 fusion.52
  166.7 2.6 %fusion.54 = f32[3072,256]{1,0:T(8,128)S(1)} fusion(f32[3072,256]{1,0:T(8,128)S(1)} %bitcast.47, f32[256,256]{1,0:T(8,128)S(1)} %copy-done.2), kind=kOutput, calls=%fused_computation.116 | convolution fusion | flops 2415919104 | bytes 6553600 | tf_op jit(solution)/shard_map/dot_general | solution.py:85
  171.4 2.6 %collective-permute-done.5 = f32[3,2,16,256]{3,2,1,0:T(8,128)S(1)} collective-permute-done((f32[3,2,16,256]{3,2,1,0:T(8,128)S(1)}, f32[3,2,16,256]{3,2,1,0:T(8,128)S(1)}, u32[]{:S(2)}, u32[]{:S(2)}) %collective-permute-start.5) | collective-permute-done | bytes 98336 | tf_op jit(solution)/shard_map/ppermute | solution.py:24
  176.0 5.0 %collective-permute-done.7 = f32[3,68,2,256]{3,2,1,0:T(2,128)S(1)} collective-permute-done((f32[3,68,2,256]{3,2,1,0:T(2,128)S(1)}, f32[3,68,2,256]{3,2,1,0:T(2,128)S(1)}, u32[]{:S(2)}, u32[]{:S(2)}) %collective-permute-start.7) | collective-permute-done | bytes 417824 | tf_op jit(solution)/shard_map/ppermute | solution.py:26
  181.0 3.1 %collective-permute-done.8 = f32[3,68,2,256]{3,2,1,0:T(2,128)S(1)} collective-permute-done((f32[3,68,2,256]{3,2,1,0:T(2,128)S(1)}, f32[3,68,2,256]{3,2,1,0:T(2,128)S(1)}, u32[]{:S(2)}, u32[]{:S(2)}) %collective-permute-start.8) | collective-permute-done | bytes 417824 | tf_op jit(solution)/shard_map/ppermute | solution.py:24
  184.1 1.3 pad_maximum_fusion.1
  185.4 5.0 %fusion.24 = f32[3,64,16,256]{3,2,1,0:T(8,128)} fusion(f32[3,68,18,256]{3,2,1,0:T(8,128)S(1)} %get-tuple-element.18, f32[3,68,18,256]{3,2,1,0:T(8,128)S(1)} %get-tuple-element.17, f32[3,64,16,256]{3,2,1,0:T(8,128)S(1)} %bitcast.41, f32[3,2,16,256]{3,2,1,0:T(8,128)} %copy-done.3, f32[3,2,16,256]{3,2,1,0:T(8,128)S(1)} %collective-permute-done.5, ...), kind=kLoop, calls=%fused_computation.57 | loop fusion | flops 18874368 | bytes 19072000 | tf_op jit(solution)/shard_map/add | solution.py:80
  190.4 2.3 fusion.50
  193.0 2.6 %fusion.55 = f32[3072,256]{1,0:T(8,128)S(1)} fusion(f32[3072,256]{1,0:T(8,128)S(1)} %bitcast.48, f32[256,256]{1,0:T(8,128)S(1)} %copy-done.2), kind=kOutput, calls=%fused_computation.117 | convolution fusion | flops 2415919104 | bytes 6553600 | tf_op jit(solution)/shard_map/dot_general | solution.py:85
  197.8 2.6 %collective-permute-done.10 = f32[3,2,16,256]{3,2,1,0:T(8,128)S(1)} collective-permute-done((f32[3,2,16,256]{3,2,1,0:T(8,128)S(1)}, f32[3,2,16,256]{3,2,1,0:T(8,128)S(1)}, u32[]{:S(2)}, u32[]{:S(2)}) %collective-permute-start.10) | collective-permute-done | bytes 98336 | tf_op jit(solution)/shard_map/ppermute | solution.py:26
  202.3 5.0 %collective-permute-done.11 = f32[3,68,2,256]{3,2,1,0:T(2,128)S(1)} collective-permute-done((f32[3,68,2,256]{3,2,1,0:T(2,128)S(1)}, f32[3,68,2,256]{3,2,1,0:T(2,128)S(1)}, u32[]{:S(2)}, u32[]{:S(2)}) %collective-permute-start.11) | collective-permute-done | bytes 417824 | tf_op jit(solution)/shard_map/ppermute | solution.py:26
  207.3 3.1 %collective-permute-done.12 = f32[3,68,2,256]{3,2,1,0:T(2,128)S(1)} collective-permute-done((f32[3,68,2,256]{3,2,1,0:T(2,128)S(1)}, f32[3,68,2,256]{3,2,1,0:T(2,128)S(1)}, u32[]{:S(2)}, u32[]{:S(2)}) %collective-permute-start.12) | collective-permute-done | bytes 417824 | tf_op jit(solution)/shard_map/ppermute | solution.py:24
  210.5 1.3 pad_maximum_fusion.2
  211.8 4.9 %fusion.18 = f32[3,64,16,256]{3,2,1,0:T(8,128)} fusion(f32[3,68,18,256]{3,2,1,0:T(8,128)S(1)} %get-tuple-element.14, f32[3,68,18,256]{3,2,1,0:T(8,128)S(1)} %get-tuple-element.13, f32[3,64,16,256]{3,2,1,0:T(8,128)S(1)} %bitcast.45, f32[3,2,16,256]{3,2,1,0:T(8,128)S(1)} %collective-permute-done.10, f32[3,2,16,256]{3,2,1,0:T(8,128)} %copy-done.4, ...), kind=kLoop, calls=%fused_computation.47 | loop fusion | flops 18874368 | bytes 19072000 | tf_op jit(solution)/shard_map/add | solution.py:80
  216.6 2.3 fusion.48
  219.3 2.6 %fusion.56 = f32[3072,256]{1,0:T(8,128)S(1)} fusion(f32[3072,256]{1,0:T(8,128)S(1)} %bitcast.46, f32[256,256]{1,0:T(8,128)S(1)} %copy-done.2), kind=kOutput, calls=%fused_computation.118 | convolution fusion | flops 2415919104 | bytes 6553600 | tf_op jit(solution)/shard_map/dot_general | solution.py:85
  224.1 2.6 %collective-permute-done.13 = f32[3,2,16,256]{3,2,1,0:T(8,128)S(1)} collective-permute-done((f32[3,2,16,256]{3,2,1,0:T(8,128)S(1)}, f32[3,2,16,256]{3,2,1,0:T(8,128)S(1)}, u32[]{:S(2)}, u32[]{:S(2)}) %collective-permute-start.13) | collective-permute-done | bytes 98336 | tf_op jit(solution)/shard_map/ppermute | solution.py:24
  228.6 5.0 %collective-permute-done.15 = f32[3,68,2,256]{3,2,1,0:T(2,128)S(1)} collective-permute-done((f32[3,68,2,256]{3,2,1,0:T(2,128)S(1)}, f32[3,68,2,256]{3,2,1,0:T(2,128)S(1)}, u32[]{:S(2)}, u32[]{:S(2)}) %collective-permute-start.15) | collective-permute-done | bytes 417824 | tf_op jit(solution)/shard_map/ppermute | solution.py:26
  233.6 3.1 %collective-permute-done.16 = f32[3,68,2,256]{3,2,1,0:T(2,128)S(1)} collective-permute-done((f32[3,68,2,256]{3,2,1,0:T(2,128)S(1)}, f32[3,68,2,256]{3,2,1,0:T(2,128)S(1)}, u32[]{:S(2)}, u32[]{:S(2)}) %collective-permute-start.16) | collective-permute-done | bytes 417824 | tf_op jit(solution)/shard_map/ppermute | solution.py:24
  236.7 1.3 pad_maximum_fusion.3
  238.0 4.1 %fusion.12 = f32[3,64,16,256]{3,2,1,0:T(8,128)} fusion(f32[3,68,18,256]{3,2,1,0:T(8,128)S(1)} %get-tuple-element.10, f32[3,68,18,256]{3,2,1,0:T(8,128)S(1)} %get-tuple-element.9, f32[3,64,16,256]{3,2,1,0:T(8,128)S(1)} %bitcast.37, f32[3,2,16,256]{3,2,1,0:T(8,128)S(1)} %collective-permute-done.14, f32[3,2,16,256]{3,2,1,0:T(8,128)S(1)} %collective-permute-done.13, ...), kind=kLoop, calls=%fused_computation.37 | loop fusion | flops 18874368 | bytes 19072000 | tf_op jit(solution)/shard_map/add | solution.py:80
  242.1 2.4 fusion.46
  244.5 4.3 %fusion.41 = f32[1,3,64,16,256]{4,3,2,1,0:T(8,128)} fusion(f32[256,256,1,1]{1,0,3,2:T(8,128)S(1)} %copy-done.5, f32[1,64,16,256]{3,2,1,0:T(8,128)S(1)} %get-tuple-element.26, f32[1,64,16,256]{3,2,1,0:T(8,128)S(1)} %get-tuple-element.27, f32[1,64,16,256]{3,2,1,0:T(8,128)S(1)} %get-tuple-element.25), kind=kOutput, calls=%fused_computation.87 | convolution fusion | flops 2417491968 | bytes 6553600 | tf_op jit(solution)/shard_map/dot_general | solution.py:85
  (53 shorter events, 18.1 us)
Async XLA Ops:
  0.0 139.1 %copy-start = (f32[1,3,64,16,256]{4,3,2,1,0:T(8,128)S(1)}, f32[1,3,64,16,256]{4,3,2,1,0:T(8,128)}, u32[]{:S(2)}) copy-start(f32[1,3,64,16,256]{4,3,2,1,0:T(8,128)} %param.8) | copy-start | bytes 9437188
  0.0 73.7 %collective-permute-start = (f32[1,3,64,16,256]{4,3,2,1,0:T(8,128)}, f32[1,3,64,16,256]{4,3,2,1,0:T(8,128)S(1)}, u32[]{:S(2)}, u32[]{:S(2)}) collective-permute-start(f32[1,3,64,16,256]{4,3,2,1,0:T(8,128)} %param.6), channel_id=1, source_target_pairs={{0,224},{32,0},{64,32},{96,64},{128,96},{160,128},{192,160},{224,1... | collective-permute-start | bytes 9437192 | tf_op jit(solution)/shard_map/ppermute | solution.py:36
  73.7 5.4 %copy-start.1 = (f32[1,3,64,16,256]{4,3,2,1,0:T(8,128)}, f32[1,3,64,16,256]{4,3,2,1,0:T(8,128)S(1)}, u32[]{:S(2)}) copy-start(f32[1,3,64,16,256]{4,3,2,1,0:T(8,128)S(1)} %collective-permute-done) | copy-start | bytes 9437188
  143.2 6.6 %copy-start.6 = (f32[256]{0:T(256)S(1)}, f32[256]{0:T(256)}, u32[]{:S(2)}) copy-start(f32[256]{0:T(256)} %param.9) | copy-start | bytes 3076
  143.2 6.6 %copy-start.7 = (f32[256]{0:T(256)S(1)}, f32[256]{0:T(256)}, u32[]{:S(2)}) copy-start(f32[256]{0:T(256)} %param.10) | copy-start | bytes 3076
  143.2 4.7 %collective-permute-start.1 = (f32[3,2,16,256]{3,2,1,0:T(8,128)S(1)}, f32[3,2,16,256]{3,2,1,0:T(8,128)S(1)}, u32[]{:S(2)}, u32[]{:S(2)}) collective-permute-start(f32[3,2,16,256]{3,2,1,0:T(8,128)S(1)} %get-tuple-element.43), channel_id=1, source_target_pairs={{0,16},{16,0},{1,17},{17,1},{2,18},{18,2},{3,19},{19,3},{4,20},{20... | collective-permute-start | bytes 294920 | tf_op jit(solution)/shard_map/ppermute | solution.py:24
  144.0 4.9 %collective-permute-start.2 = (f32[3,2,16,256]{3,2,1,0:T(8,128)S(1)}, f32[3,2,16,256]{3,2,1,0:T(8,128)S(1)}, u32[]{:S(2)}, u32[]{:S(2)}) collective-permute-start(f32[3,2,16,256]{3,2,1,0:T(8,128)S(1)} %get-tuple-element.44), channel_id=1, source_target_pairs={{16,0},{0,16},{17,1},{1,17},{18,2},{2,18},{19,3},{3,19},{20,4},{4,... | collective-permute-start | bytes 294920 | tf_op jit(solution)/shard_map/ppermute | solution.py:26
  149.3 5.6 %collective-permute-start.3 = (f32[3,68,2,256]{3,2,1,0:T(2,128)S(1)}, f32[3,68,2,256]{3,2,1,0:T(2,128)S(1)}, u32[]{:S(2)}, u32[]{:S(2)}) collective-permute-start(f32[3,68,2,256]{3,2,1,0:T(2,128)S(1)} %get-tuple-element.23), channel_id=1, source_target_pairs={{1,0},{2,1},{3,2},{4,3},{5,4},{6,5},{7,6},{8,7},{9,8},{10,9},{11,1... | collective-permute-start | bytes 1253384 | tf_op jit(solution)/shard_map/ppermute | solution.py:26
  149.3 8.7 %collective-permute-start.4 = (f32[3,68,2,256]{3,2,1,0:T(2,128)S(1)}, f32[3,68,2,256]{3,2,1,0:T(2,128)S(1)}, u32[]{:S(2)}, u32[]{:S(2)}) collective-permute-start(f32[3,68,2,256]{3,2,1,0:T(2,128)S(1)} %get-tuple-element.24), channel_id=1, source_target_pairs={{0,1},{1,2},{2,3},{3,4},{4,5},{5,6},{6,7},{7,8},{8,9},{9,10},{10,1... | collective-permute-start | bytes 1253384 | tf_op jit(solution)/shard_map/ppermute | solution.py:24
  165.7 1.0 copy-start.2
  169.3 4.7 %collective-permute-start.5 = (f32[3,2,16,256]{3,2,1,0:T(8,128)S(1)}, f32[3,2,16,256]{3,2,1,0:T(8,128)S(1)}, u32[]{:S(2)}, u32[]{:S(2)}) collective-permute-start(f32[3,2,16,256]{3,2,1,0:T(8,128)S(1)} %get-tuple-element.38), channel_id=1, source_target_pairs={{0,16},{16,0},{1,17},{17,1},{2,18},{18,2},{3,19},{19,3},{4,20},{20... | collective-permute-start | bytes 294920 | tf_op jit(solution)/shard_map/ppermute | solution.py:24
  170.4 4.7 %collective-permute-start.6 = (f32[3,2,16,256]{3,2,1,0:T(8,128)S(1)}, f32[3,2,16,256]{3,2,1,0:T(8,128)S(1)}, u32[]{:S(2)}, u32[]{:S(2)}) collective-permute-start(f32[3,2,16,256]{3,2,1,0:T(8,128)S(1)} %get-tuple-element.39), channel_id=1, source_target_pairs={{16,0},{0,16},{17,1},{1,17},{18,2},{2,18},{19,3},{3,19},{20,4},{4,... | collective-permute-start | bytes 294920 | tf_op jit(solution)/shard_map/ppermute | solution.py:26
  175.1 10.3 %copy-start.3 = (f32[3,2,16,256]{3,2,1,0:T(8,128)}, f32[3,2,16,256]{3,2,1,0:T(8,128)S(1)}, u32[]{:S(2)}) copy-start(f32[3,2,16,256]{3,2,1,0:T(8,128)S(1)} %collective-permute-done.6) | copy-start | bytes 294916
  175.4 5.6 %collective-permute-start.7 = (f32[3,68,2,256]{3,2,1,0:T(2,128)S(1)}, f32[3,68,2,256]{3,2,1,0:T(2,128)S(1)}, u32[]{:S(2)}, u32[]{:S(2)}) collective-permute-start(f32[3,68,2,256]{3,2,1,0:T(2,128)S(1)} %get-tuple-element.19), channel_id=1, source_target_pairs={{1,0},{2,1},{3,2},{4,3},{5,4},{6,5},{7,6},{8,7},{9,8},{10,9},{11,1... | collective-permute-start | bytes 1253384 | tf_op jit(solution)/shard_map/ppermute | solution.py:26
  175.4 8.7 %collective-permute-start.8 = (f32[3,68,2,256]{3,2,1,0:T(2,128)S(1)}, f32[3,68,2,256]{3,2,1,0:T(2,128)S(1)}, u32[]{:S(2)}, u32[]{:S(2)}) collective-permute-start(f32[3,68,2,256]{3,2,1,0:T(2,128)S(1)} %get-tuple-element.20), channel_id=1, source_target_pairs={{0,1},{1,2},{2,3},{3,4},{4,5},{5,6},{6,7},{7,8},{8,9},{9,10},{10,1... | collective-permute-start | bytes 1253384 | tf_op jit(solution)/shard_map/ppermute | solution.py:24
  195.7 4.7 %collective-permute-start.10 = (f32[3,2,16,256]{3,2,1,0:T(8,128)S(1)}, f32[3,2,16,256]{3,2,1,0:T(8,128)S(1)}, u32[]{:S(2)}, u32[]{:S(2)}) collective-permute-start(f32[3,2,16,256]{3,2,1,0:T(8,128)S(1)} %get-tuple-element.34), channel_id=1, source_target_pairs={{16,0},{0,16},{17,1},{1,17},{18,2},{2,18},{19,3},{3,19},{20,4},{4,... | collective-permute-start | bytes 294920 | tf_op jit(solution)/shard_map/ppermute | solution.py:26
  196.8 4.7 %collective-permute-start.9 = (f32[3,2,16,256]{3,2,1,0:T(8,128)S(1)}, f32[3,2,16,256]{3,2,1,0:T(8,128)S(1)}, u32[]{:S(2)}, u32[]{:S(2)}) collective-permute-start(f32[3,2,16,256]{3,2,1,0:T(8,128)S(1)} %get-tuple-element.33), channel_id=1, source_target_pairs={{0,16},{16,0},{1,17},{17,1},{2,18},{18,2},{3,19},{19,3},{4,20},{20... | collective-permute-start | bytes 294920 | tf_op jit(solution)/shard_map/ppermute | solution.py:24
  201.4 10.3 %copy-start.4 = (f32[3,2,16,256]{3,2,1,0:T(8,128)}, f32[3,2,16,256]{3,2,1,0:T(8,128)S(1)}, u32[]{:S(2)}) copy-start(f32[3,2,16,256]{3,2,1,0:T(8,128)S(1)} %collective-permute-done.9) | copy-start | bytes 294916
  201.7 5.6 %collective-permute-start.11 = (f32[3,68,2,256]{3,2,1,0:T(2,128)S(1)}, f32[3,68,2,256]{3,2,1,0:T(2,128)S(1)}, u32[]{:S(2)}, u32[]{:S(2)}) collective-permute-start(f32[3,68,2,256]{3,2,1,0:T(2,128)S(1)} %get-tuple-element.15), channel_id=1, source_target_pairs={{1,0},{2,1},{3,2},{4,3},{5,4},{6,5},{7,6},{8,7},{9,8},{10,9},{11,1... | collective-permute-start | bytes 1253384 | tf_op jit(solution)/shard_map/ppermute | solution.py:26
  201.8 8.7 %collective-permute-start.12 = (f32[3,68,2,256]{3,2,1,0:T(2,128)S(1)}, f32[3,68,2,256]{3,2,1,0:T(2,128)S(1)}, u32[]{:S(2)}, u32[]{:S(2)}) collective-permute-start(f32[3,68,2,256]{3,2,1,0:T(2,128)S(1)} %get-tuple-element.16), channel_id=1, source_target_pairs={{0,1},{1,2},{2,3},{3,4},{4,5},{5,6},{6,7},{7,8},{8,9},{9,10},{10,1... | collective-permute-start | bytes 1253384 | tf_op jit(solution)/shard_map/ppermute | solution.py:24
  221.9 4.7 %collective-permute-start.13 = (f32[3,2,16,256]{3,2,1,0:T(8,128)S(1)}, f32[3,2,16,256]{3,2,1,0:T(8,128)S(1)}, u32[]{:S(2)}, u32[]{:S(2)}) collective-permute-start(f32[3,2,16,256]{3,2,1,0:T(8,128)S(1)} %get-tuple-element.28), channel_id=1, source_target_pairs={{0,16},{16,0},{1,17},{17,1},{2,18},{18,2},{3,19},{19,3},{4,20},{20... | collective-permute-start | bytes 294920 | tf_op jit(solution)/shard_map/ppermute | solution.py:24
  223.0 4.7 %collective-permute-start.14 = (f32[3,2,16,256]{3,2,1,0:T(8,128)S(1)}, f32[3,2,16,256]{3,2,1,0:T(8,128)S(1)}, u32[]{:S(2)}, u32[]{:S(2)}) collective-permute-start(f32[3,2,16,256]{3,2,1,0:T(8,128)S(1)} %get-tuple-element.29), channel_id=1, source_target_pairs={{16,0},{0,16},{17,1},{1,17},{18,2},{2,18},{19,3},{3,19},{20,4},{4,... | collective-permute-start | bytes 294920 | tf_op jit(solution)/shard_map/ppermute | solution.py:26
  228.0 5.6 %collective-permute-start.15 = (f32[3,68,2,256]{3,2,1,0:T(2,128)S(1)}, f32[3,68,2,256]{3,2,1,0:T(2,128)S(1)}, u32[]{:S(2)}, u32[]{:S(2)}) collective-permute-start(f32[3,68,2,256]{3,2,1,0:T(2,128)S(1)} %get-tuple-element.11), channel_id=1, source_target_pairs={{1,0},{2,1},{3,2},{4,3},{5,4},{6,5},{7,6},{8,7},{9,8},{10,9},{11,1... | collective-permute-start | bytes 1253384 | tf_op jit(solution)/shard_map/ppermute | solution.py:26
  228.0 8.7 %collective-permute-start.16 = (f32[3,68,2,256]{3,2,1,0:T(2,128)S(1)}, f32[3,68,2,256]{3,2,1,0:T(2,128)S(1)}, u32[]{:S(2)}, u32[]{:S(2)}) collective-permute-start(f32[3,68,2,256]{3,2,1,0:T(2,128)S(1)} %get-tuple-element.12), channel_id=1, source_target_pairs={{0,1},{1,2},{2,3},{3,4},{4,5},{5,6},{6,7},{7,8},{8,9},{9,10},{10,1... | collective-permute-start | bytes 1253384 | tf_op jit(solution)/shard_map/ppermute | solution.py:24
  242.1 2.4 copy-start.5
where the time goes:
time: 249 us
  waiting for transfers between devices  120 us (48%)
  blocking collectives  58.7 us (24%)
  other arithmetic  44.1 us (18%)
  matrix products  12.1 us (5%)
  starting transfers between devices  10.8 us (4%)
    ppermute x1, waiting for transfers between devices, from_behind(): return lax.ppermute(value, axis, pairs)  73.3 us
    psum x1, blocking collectives, shards(): lax.psum((jnp.sum(started * direction), jnp.sum(direction * direction)),...  58.7 us
    ppermute x8, waiting for transfers between devices, with_halo(): lax.ppermute(head, axis, [((i + 1) % count, i) for i in range(count)])  25.7 us
    ppermute x8, waiting for transfers between devices, with_halo(): lax.ppermute(tail, axis, [(i, (i + 1) % count) for i in range(count)])  21.4 us
    add x4, other arithmetic, advance(): center + TIME_STEP * velocity * advect + DIFFUSE * (lap_x + lap_z)  18 us
    dot_general x4, matrix products, advance(): jnp.dot(flattened, table_t, precision=lax.Precision.HIGHEST, preferred_el...  12.1 us
    slice x4, other arithmetic, advance(): explicit[:1]  9.38 us
    ppermute x8, starting transfers between devices, with_halo(): lax.ppermute(tail, axis, [(i, (i + 1) % count) for i in range(count)])  5.99 us
  transfers between devices with their start and end apart: 17, of which 17 were waited for; matrix products, arithmetic and copies ran while one was open for 0% of the time, Pallas kernels for 0%

commit v1 on v0

v1 whole, which is shorter than its diff:
```python
import functools

import jax
import jax.numpy as jnp
import ml_dtypes
import numpy as np
from jax import lax
from jax.experimental import pallas as pl
from jax.experimental.pallas import tpu as pltpu
from jax.sharding import PartitionSpec as P

TIME_STEP = 0.15
DIFFUSE = 0.1
WALL_COEF = 0.0002
EPSILON = 1e-06
NEWTON_TURNS = 100
MESH = pl.DeviceIdType.MESH

NCOMP = 3
CX = 64
CZ = 16
LANES = 128
HALO = 8
XB = 16
NXO = CX + 2 * HALO
NXB = NXO + 4
ZIN = 40
ZBUF = 32
ZOUT = (32, 24, 24, 16)
CHUNK = 8
NCH = CX // CHUNK


def invert_newton(matrix):
    order = matrix.shape[0]
    identity = np.eye(order)
    scale_one = np.max(np.sum(np.abs(matrix), axis=0))
    scale_inf = np.max(np.sum(np.abs(matrix), axis=1))
    approx = matrix.T / (scale_one * scale_inf)
    for turn_index in range(NEWTON_TURNS):
        approx = approx @ (2.0 * identity - matrix @ approx)
    return approx


def wall_table(points):
    intervals = points - 1
    cheb_nodes = np.cos(np.pi * np.arange(points) / intervals)
    weights = np.ones(points)
    weights[0] = 2.0
    weights[-1] = 2.0
    weights = weights * (-1.0) ** np.arange(points)
    spread = cheb_nodes[:, None] - cheb_nodes[None, :]
    first_deriv = weights[:, None] / weights[None, :] / (spread + np.eye(points))
    first_deriv = first_deriv - np.eye(points) * first_deriv.sum(axis=1)[:, None]
    second = first_deriv @ first_deriv
    interior = np.eye(points - 2) - WALL_COEF * second[1:-1, 1:-1]
    helm_table = np.zeros((points, points))
    helm_table[1:-1, 1:-1] = invert_newton(interior)
    return helm_table.T.astype(np.float32)


def kernel(
    sizes,
    t_hbm, j_hbm, tan_hbm, coef_ref, hhi_ref, hlo_ref,
    out_hbm,
    tb, b0, w1, w2, w3, res, osend, orecv, ehi, elo, acc, ar_send, ar_recv_a, ar_mid, ar_recv_b,
    load_sem, t_send, t_recv, zs_send, zs_recv, zt_send, zt_recv,
    ra_send, ra_recv, rb_send, rb_recv, o_send, o_recv, out_sem,
):
    nseg, ngx, ngz = sizes
    seg, gx, gz = lax.axis_index("seg"), lax.axis_index("gx"), lax.axis_index("gz")
    nz = ngz // 2
    zc, core = gz // 2, lax.rem(gz, 2)
    before, after = lax.rem(seg + nseg - 1, nseg), lax.rem(seg + 1, nseg)
    zl, zr = lax.rem(gz + ngz - 1, ngz), lax.rem(gz + 1, ngz)
    ogx, ogz = 1 - gx, zc * 2 + (1 - core)
    left, right, partner = (seg, gx, zl), (seg, gx, zr), (seg, ogx, gz)
    group_a = [(seg, gx, ogz), (seg, ogx, gz), (seg, ogx, ogz)]
    group_b = [(seg, gx, lax.rem(zc + o, nz) * 2 + core) for o in range(1, nz)]
    outer = (seg, gx, lax.rem(gz + jnp.where(core == 0, ngz - 1, 1), ngz))

    def loads(start):
        for a, src in ((0, tan_hbm), (1, j_hbm)):
            for c in range(NCOMP):
                for h in range(2):
                    cp = pltpu.make_async_copy(
                        src.at[0, c, :, :, pl.ds(h * LANES, LANES)],
                        b0.at[a * NCOMP + c, h, pl.ds(2 + HALO, CX), pl.ds(HALO, CZ), :],
                        load_sem.at[(a * NCOMP + c) * 2 + h],
                    )
                    if start:
                        cp.start()
                    else:
                        cp.wait()

    loads(True)

    barrier = pltpu.get_barrier_semaphore()
    peers = [(before, gx, gz), (after, gx, gz), outer] + group_a + group_b
    for d in peers:
        pl.semaphore_signal(barrier, inc=1, device_id=d, device_id_type=MESH)
    pl.semaphore_wait(barrier, len(peers))

    def t_copy(c, i):
        rows = pl.ds(i * CHUNK, CHUNK)
        return pltpu.make_async_remote_copy(
            src_ref=t_hbm.at[0, c, rows],
            dst_ref=tb.at[c, rows],
            send_sem=t_send.at[c * NCH + i],
            recv_sem=t_recv.at[c * NCH + i],
            device_id=(before, gx, gz),
            device_id_type=MESH,
        )

    for c in range(NCOMP):
        @pl.loop(0, NCH)
        def _(i):
            t_copy(c, i).start()

    def zero_pads(s, _):
        for h in range(2):
            for lo, hi in ((0, 2 + HALO), (2 + HALO + CX, NXB)):
                b0[s, h, lo:hi, :, :] = jnp.zeros((hi - lo, ZIN, LANES), jnp.float32)
            b0[s, h, 2 + HALO:2 + HALO + CX, 2 * HALO + CZ:, :] = jnp.zeros(
                (CX, ZIN - 2 * HALO - CZ, LANES), jnp.float32)
        return 0

    lax.fori_loop(0, 2 * NCOMP, zero_pads, 0)
    for w in (w1, w2, w3):
        for s in range(2):
            for h in range(2):
                for lo in (0, NXB - 2):
                    w[s, h, lo:lo + 2, :, :] = jnp.zeros((2, ZBUF, LANES), jnp.float32)
                w[s, h, 2:NXB - 2, 24:, :] = jnp.zeros((NXB - 4, 8, LANES), jnp.float32)
    acc[...] = jnp.zeros_like(acc)

    def strip(slot, x0, nx, side, send_sem, recv_sem):
        rows = pl.ds(2 + HALO + x0, nx)
        src = pl.ds(HALO, HALO) if side == 0 else pl.ds(HALO + CZ - HALO, HALO)
        dst = pl.ds(HALO + CZ, HALO) if side == 0 else pl.ds(0, HALO)
        return pltpu.make_async_remote_copy(
            src_ref=b0.at[slot, :, rows, src, :],
            dst_ref=b0.at[slot, :, rows, dst, :],
            send_sem=send_sem,
            recv_sem=recv_sem,
            device_id=left if side == 0 else right,
            device_id_type=MESH,
        )

    def tan_strip(c, side):
        k = c * 2 + side
        return strip(c, 0, CX, side, zs_send.at[k], zs_recv.at[k])

    def start_strip(c, i, side):
        k = (c * NCH + i) * 2 + side
        return strip(NCOMP + c, i * CHUNK, CHUNK, side, zt_send.at[k], zt_recv.at[k])

    loads(False)
    for c in range(NCOMP):
        for side in range(2):
            tan_strip(c, side).start()

    def dot_rows(first, second):
        prod = first * second
        return jnp.sum(prod.reshape(-1, 8, LANES), axis=0)

    def square(i, _):
        c, x = i // NCH, lax.rem(i, NCH) * CHUNK
        for h in range(2):
            tau = b0[c, h, pl.ds(2 + HALO + x, CHUNK), HALO:HALO + CZ, :]
            acc[1] += dot_rows(tau, tau)
        return 0

    lax.fori_loop(0, NCOMP * NCH, square, 0)

    def arrive(c):
        def piece(i, _):
            t_copy(c, i).wait_recv()
            rows = pl.ds(2 + HALO + i * CHUNK, CHUNK)
            for h in range(2):
                started = b0[NCOMP + c, h, rows, HALO:HALO + CZ, :] + tb[
                    c, pl.ds(i * CHUNK, CHUNK), :, h * LANES:(h + 1) * LANES]
                b0[NCOMP + c, h, rows, HALO:HALO + CZ, :] = started
                acc[0] += dot_rows(started, b0[c, h, rows, HALO:HALO + CZ, :])
            start_strip(c, i, 0).start()
            start_strip(c, i, 1).start()
            return 0

        lax.fori_loop(0, NCH, piece, 0)

    def reduce_a(o):
        return pltpu.make_async_remote_copy(
            src_ref=ar_send, dst_ref=ar_recv_a.at[o], send_sem=ra_send.at[o], recv_sem=ra_recv.at[o],
            device_id=group_a[o], device_id_type=MESH)

    def reduce_b(o):
        return pltpu.make_async_remote_copy(
            src_ref=ar_mid, dst_ref=ar_recv_b.at[o], send_sem=rb_send.at[o], recv_sem=rb_recv.at[o],
            device_id=group_b[o], device_id_type=MESH)

    def outflow(c):
        return pltpu.make_async_remote_copy(
            src_ref=osend.at[c], dst_ref=orecv.at[c], send_sem=o_send.at[c], recv_sem=o_recv.at[c],
            device_id=partner, device_id_type=MESH)

    def reduce_all():
        row = lax.broadcasted_iota(jnp.int32, (8, LANES), 0)
        top = jnp.sum(acc[0], axis=0, keepdims=True)
        low = jnp.sum(acc[1], axis=0, keepdims=True)
        ar_send[...] = jnp.where(row == 0, top, jnp.where(row == 1, low, 0.0))
        for o in range(3):
            reduce_a(o).start()
        for o in range(3):
            reduce_a(o).wait_recv()
        ar_mid[...] = ar_send[...] + ar_recv_a[0] + (ar_recv_a[1] + ar_recv_a[2])
        for o in range(nz - 1):
            reduce_b(o).start()
        for o in range(nz - 1):
            reduce_b(o).wait_recv()
        total = ar_mid[...]
        for o in range(nz - 1):
            total += ar_recv_b[o]
        sums = jnp.sum(total, axis=1, keepdims=True)
        acc[0] = jnp.broadcast_to(sums[0:1] / (sums[1:2] + EPSILON), (8, LANES))

    def send_outflow(c):
        along = acc[0, 0:1, 0:1]

        def put(i, _):
            osend[c, 0, i] = res[1, c, HALO + CX + i] - along * res[0, c, HALO + CX + i]
            osend[c, 1, i] = res[1, c, i] - along * res[0, c, i]
            return 0

        lax.fori_loop(0, HALO, put, 0)
        outflow(c).start()

    bufs = (b0, w1, w2, w3)

    def step(k, n, a, c):
        half_set = jnp.minimum(c, 1)
        z = ZOUT[k]
        src = bufs[k]
        slot = n if k == 0 else half_set
        slot0 = a * NCOMP if k == 0 else 0
        sheared = jnp.where(c == 1, 1.0, 0.0).astype(jnp.float32)

        def block(b, _):
            for p in range(XB // 2):
                for h in range(2):
                    cs = [coef_ref[r:r + 1, h * LANES:(h + 1) * LANES] for r in range(5)]
                    shear = cs[4] * sheared
                    both = []
                    for q in range(2):
                        i = b * XB + 2 * p + q

                        def at(dx, dz):
                            return src[slot, h, i + 2 + dx, 2 + dz:2 + dz + z, :]

                        e = 0.5 * at(0, 0)
                        e += (DIFFUSE * 16.0 / 12.0) * (at(0, 1) + at(0, -1))
                        e += (-DIFFUSE / 12.0) * (at(0, 2) + at(0, -2))
                        e += cs[0] * at(1, 0) + cs[1] * at(-1, 0)
                        e += cs[2] * at(2, 0) + cs[3] * at(-2, 0)
                        e += shear * src[slot0, h, i + 2, 2:2 + z, :]
                        both.append(e)
                    e = jnp.concatenate(both, axis=0)
                    hi = e.astype(jnp.bfloat16)
                    lo = (e - hi.astype(jnp.float32)).astype(jnp.bfloat16)
                    ehi[2 * p * z:2 * (p + 1) * z, h * LANES:(h + 1) * LANES] = hi
                    elo[2 * p * z:2 * (p + 1) * z, h * LANES:(h + 1) * LANES] = lo
            m = XB * z
            out = jnp.dot(ehi[:m], hhi_ref[...], preferred_element_type=jnp.float32)
            out += jnp.dot(elo[:m], hhi_ref[...], preferred_element_type=jnp.float32)
            out += jnp.dot(ehi[:m], hlo_ref[...], preferred_element_type=jnp.float32)
            if k < 3:
                dst = bufs[k + 1]
                for h in range(2):
                    dst[half_set, h, pl.ds(2 + b * XB, XB), 0:z, :] = out[
                        :, h * LANES:(h + 1) * LANES].reshape(XB, z, LANES)
            else:
                res[a, c, pl.ds(b * XB, XB)] = out.reshape(XB, z, 2 * LANES)
            return 0

        lax.fori_loop(0, NXO // XB, block, 0)

    def item(n, _):
        a, c = n // NCOMP, lax.rem(n, NCOMP)

        @pl.when(a == 0)
        def _():
            for side in range(2):
                tan_strip(c, side).wait_recv()

        @pl.when(a == 1)
        def _():
            arrive(c)

        @pl.when(n == 2 * NCOMP - 1)
        def _():
            reduce_all()
            for d in range(NCOMP - 1):
                send_outflow(d)

        @pl.when(a == 1)
        def _():
            def strips(i, _):
                start_strip(c, i, 0).wait_recv()
                start_strip(c, i, 1).wait_recv()
                return 0

            lax.fori_loop(0, NCH, strips, 0)

        for k in range(4):
            step(k, n, a, c)
        return 0

    lax.fori_loop(0, 2 * NCOMP, item, 0)
    send_outflow(NCOMP - 1)

    along = acc[0, 0:1, 0:1]

    def write(c, lo, n, k):
        return pltpu.make_async_copy(
            tb.at[c, pl.ds(lo, n)], out_hbm.at[0, c, pl.ds(lo, n)], out_sem.at[c * 3 + k])

    inner = CX - 2 * HALO
    for c in range(NCOMP):
        def mix(i, _):
            tb[c, HALO + i] = res[1, c, 2 * HALO + i] - along * res[0, c, 2 * HALO + i]
            return 0

        lax.fori_loop(0, inner, mix, 0)
        write(c, HALO, inner, 0).start()
    for c in range(NCOMP):
        outflow(c).wait_recv()

        def edges(i, _):
            for side, at in ((0, 0), (1, CX - HALO)):
                own = res[1, c, HALO + at + i] - along * res[0, c, HALO + at + i]
                tb[c, at + i] = own + orecv[c, side, i]
            return 0

        lax.fori_loop(0, HALO, edges, 0)
        write(c, 0, HALO, 1).start()
        write(c, CX - HALO, HALO, 2).start()

    for c in range(NCOMP):
        write(c, HALO, inner, 0).wait()
        write(c, 0, HALO, 1).wait()
        write(c, CX - HALO, HALO, 2).wait()
        outflow(c).wait_send()
        for side in range(2):
            tan_strip(c, side).wait_send()

        @pl.loop(0, NCH)
        def _(i):
            t_copy(c, i).wait_send()
            start_strip(c, i, 0).wait_send()
            start_strip(c, i, 1).wait_send()
    for o in range(3):
        reduce_a(o).wait_send()
    for o in range(nz - 1):
        reduce_b(o).wait_send()


def shards(sizes, terminal, jump, tangent, base_velocity, base_shear):
    table = wall_table(base_velocity.shape[0])
    high = table.astype(ml_dtypes.bfloat16)
    low = (table - high.astype(np.float32)).astype(ml_dtypes.bfloat16)
    near, far = DIFFUSE * 16.0 / 12.0, DIFFUSE / 12.0
    push = TIME_STEP * base_velocity
    coefs = jnp.stack(
        [
            push * (8.0 / 12.0) + near,
            push * (-8.0 / 12.0) + near,
            push * (-1.0 / 12.0) - far,
            push * (1.0 / 12.0) - far,
            -TIME_STEP * base_shear,
        ]
        + [jnp.zeros_like(push)] * 3
    )
    nz = sizes[2] // 2
    f32 = jnp.float32
    dma = pltpu.SemaphoreType.DMA
    hbm = pl.BlockSpec(memory_space=pl.ANY)
    vmem = pl.BlockSpec(memory_space=pltpu.VMEM)
    lanes2 = 2 * LANES
    return pl.pallas_call(
        functools.partial(kernel, sizes),
        out_shape=jax.ShapeDtypeStruct(terminal.shape, f32),
        in_specs=[hbm, hbm, hbm, vmem, vmem, vmem],
        out_specs=hbm,
        scratch_shapes=[
            pltpu.VMEM((NCOMP, CX, CZ, lanes2), f32),
            pltpu.VMEM((2 * NCOMP, 2, NXB, ZIN, LANES), f32),
            pltpu.VMEM((2, 2, NXB, ZBUF, LANES), f32),
            pltpu.VMEM((2, 2, NXB, ZBUF, LANES), f32),
            pltpu.VMEM((2, 2, NXB, ZBUF, LANES), f32),
            pltpu.VMEM((2, NCOMP, NXO, CZ, lanes2), f32),
            pltpu.VMEM((NCOMP, 2, HALO, CZ, lanes2), f32),
            pltpu.VMEM((NCOMP, 2, HALO, CZ, lanes2), f32),
            pltpu.VMEM((XB * ZBUF, lanes2), jnp.bfloat16),
            pltpu.VMEM((XB * ZBUF, lanes2), jnp.bfloat16),
            pltpu.VMEM((2, 8, LANES), f32),
            pltpu.VMEM((8, LANES), f32),
            pltpu.VMEM((3, 8, LANES), f32),
            pltpu.VMEM((8, LANES), f32),
            pltpu.VMEM((nz - 1, 8, LANES), f32),
            dma((4 * NCOMP,)),
            dma((NCOMP * NCH,)),
            dma((NCOMP * NCH,)),
            dma((NCOMP * 2,)),
            dma((NCOMP * 2,)),
            dma((NCOMP * NCH * 2,)),
            dma((NCOMP * NCH * 2,)),
            dma((3,)),
            dma((3,)),
            dma((nz - 1,)),
            dma((nz - 1,)),
            dma((NCOMP,)),
            dma((NCOMP,)),
            dma((3 * NCOMP,)),
        ],
        compiler_params=pltpu.CompilerParams(
            collective_id=0, has_side_effects=True, vmem_limit_bytes=58 * 1024 * 1024
        ),
    )(terminal, jump, tangent, coefs, jnp.asarray(high), jnp.asarray(low))


def solution(mesh):
    sizes = tuple(mesh.shape[name] for name in ("seg", "gx", "gz"))
    split = P("seg", None, "gx", "gz", None)
    return jax.shard_map(
        functools.partial(shards, sizes),
        mesh=mesh,
        in_specs=(split, split, split, P(), P()),
        out_specs=split,
        check_vma=False,
    )
```

time: 249 us -> 125 us (0.50)
  waiting for transfers between devices: 120 us -> 0 us
  Pallas kernels: 0 us -> 118 us
  blocking collectives: 58.7 us -> 0 us
  other arithmetic: 44.1 us -> 1.36 us
  matrix products: 12.1 us -> 0 us
  starting transfers between devices: 10.8 us -> 0 us
  local copies, waits for them, and re-layouts: 0.93 us -> 4.48 us
    ppermute x17 -> x0, waiting for transfers between devices: 120 us -> none  [the longest x1 73.3 us: from_behind(): return lax.ppermute(value, axis, pairs)]
    pallas_call x0 -> x1, Pallas kernels: none -> 118 us  [shards(): pl.pallas_call(functools.partial(kernel, sizes), out_shape=jax.ShapeDtype...]
    psum x1 -> x0, blocking collectives: 58.7 us -> none  [shards(): lax.psum((jnp.sum(started * direction), jnp.sum(direction * direction)),...]
    add x4 -> x0, other arithmetic: 18 us -> none  [advance(): center + TIME_STEP * velocity * advect + DIFFUSE * (lap_x + lap_z)]
    dot_general x4 -> x0, matrix products: 12.1 us -> none  [advance(): jnp.dot(flattened, table_t, precision=lax.Precision.HIGHEST, preferred_el...]
    ppermute x17 -> x0, starting transfers between devices: 10.8 us -> none  [the longest x8 5.99 us: with_halo(): lax.ppermute(tail, axis, [(i, (i + 1) % count) for i in range(count)])]
    slice x8 -> x0, other arithmetic: 10.5 us -> none  [the longest x4 9.38 us: advance(): explicit[:1]]
    concatenate x7 -> x0, other arithmetic: 6.11 us -> none  [the longest x4 5.19 us: with_halo(): jnp.concatenate([lax.ppermute(tail, axis, [(i, (i + 1) % count) for i in...]
  transfers between devices with their start and end apart: 17 -> 0, of which waited for: 17 -> 0; matrix products, arithmetic and copies ran while one was open for 0% -> 0% of each run, Pallas kernels for 0% -> 0%
where the time goes in v1:
time: 125 us; the launch traced here: 124 us
  Pallas kernels  118 us (94%)
  local copies, waits for them, and re-layouts  4.48 us (4%)
  other arithmetic  1.36 us (1%)
    pallas_call x1, Pallas kernels, shards(): pl.pallas_call(functools.partial(kernel, sizes), out_shape=jax.ShapeDtype...  118 us
    unnamed x1, local copies, waits for them, and re-layouts  3.86 us

profile of v1, /device:TPU:22, one launch (start us, length us, event | category | flops | bytes accessed | tf_op | source)
XLA Modules:
  0.0 123.8 jit_solution(8748347578187518544)
XLA Ops:
  0.0 0.7 broadcast_multiply_fusion
  0.7 0.7 multiply_add_fusion
  1.4 0.6 stack.27.coef_ref
  2.0 118.0 %shard_map.73 = f32[1,3,64,16,256]{4,3,2,1,0:T(8,128)} custom-call(f32[1,3,64,16,256]{4,3,2,1,0:T(8,128)} %t_hbm.1, f32[1,3,64,16,256]{4,3,2,1,0:T(8,128)} %j_hbm.1, f32[1,3,64,16,256]{4,3,2,1,0:T(8,128)} %tan_hbm.1, f32[8,256]{1,0:T(8,128)} %stack.27.coef_ref, bf16[256,256]{1,0:T(8,128)(2,1)} %constant.28.clone.hhi_ref, bf16[256,256]{1,0:T(8,128)(2,1)} %constant.29.clone.hlo_ref), custom_call_target="tpu_custom_call" | custom-call | tf_op jit(solution)/shard_map/pallas_call | solution.py:388
  120.0 3.9 %copy.9 = f32[1,3,64,16,256]{4,3,2,1,0:T(8,128)} copy(f32[1,3,64,16,256]{4,3,2,1,0:T(8,128)} %shard_map.73) | data formatting | bytes 6291456
  (2 shorter events, 0.0 us)

commit v2 on v1

--- a/solution.py
+++ b/solution.py
@@ -29,6 +29,7 @@
 ZOUT = (32, 24, 24, 16)
 CHUNK = 8
 NCH = CX // CHUNK
+AHEAD = 5
 
 
 def invert_newton(matrix):
@@ -61,11 +62,11 @@
 
 def kernel(
     sizes,
-    t_hbm, j_hbm, tan_hbm, coef_ref, hhi_ref, hlo_ref,
+    t_hbm, j_hbm, tan_hbm, vel_hbm, shear_hbm, hhi_hbm, hlo_hbm,
     out_hbm,
-    tb, b0, w1, w2, w3, res, osend, orecv, ehi, elo, acc, ar_send, ar_recv_a, ar_mid, ar_recv_b,
-    load_sem, t_send, t_recv, zs_send, zs_recv, zt_send, zt_recv,
-    ra_send, ra_recv, rb_send, rb_recv, o_send, o_recv, out_sem,
+    tb, b0, w1, w2, w3, res, osend, orecv, oraw, ehi, elo, vel_ref, shear_ref, hhi_ref, hlo_ref, coef_ref, acc, ar_send, ar_recv_a, ar_mid, ar_recv_b,
+    load_sem, const_sem, t_send, t_recv, zs_send, zs_recv, zt_send, zt_recv,
+    ra_send, ra_recv, rb_send, rb_recv, o_send, o_recv, or_send, or_recv, out_sem,
 ):
     nseg, ngx, ngz = sizes
     seg, gx, gz = lax.axis_index("seg"), lax.axis_index("gx"), lax.axis_index("gz")
@@ -80,6 +81,14 @@
     outer = (seg, gx, lax.rem(gz + jnp.where(core == 0, ngz - 1, 1), ngz))
 
     def loads(start):
+        for i, (src, dst) in enumerate((
+            (vel_hbm, vel_ref), (shear_hbm, shear_ref), (hhi_hbm, hhi_ref), (hlo_hbm, hlo_ref),
+        )):
+            cp = pltpu.make_async_copy(src, dst, const_sem.at[i])
+            if start:
+                cp.start()
+            else:
+                cp.wait()
         for a, src in ((0, tan_hbm), (1, j_hbm)):
             for c in range(NCOMP):
                 for h in range(2):
@@ -93,12 +102,11 @@
                     else:
                         cp.wait()
 
-    loads(True)
-
     barrier = pltpu.get_barrier_semaphore()
     peers = [(before, gx, gz), (after, gx, gz), outer] + group_a + group_b
     for d in peers:
         pl.semaphore_signal(barrier, inc=1, device_id=d, device_id_type=MESH)
+    loads(True)
     pl.semaphore_wait(barrier, len(peers))
 
     def t_copy(c, i):
@@ -112,10 +120,8 @@
             device_id_type=MESH,
         )
 
-    for c in range(NCOMP):
-        @pl.loop(0, NCH)
-        def _(i):
-            t_copy(c, i).start()
+    for i in range(AHEAD):
+        t_copy(i // NCH, i % NCH).start()
 
     def zero_pads(s, _):
         for h in range(2):
@@ -133,7 +139,6 @@
                     w[s, h, lo:lo + 2, :, :] = jnp.zeros((2, ZBUF, LANES), jnp.float32)
                 w[s, h, 2:NXB - 2, 24:, :] = jnp.zeros((NXB - 4, 8, LANES), jnp.float32)
     acc[...] = jnp.zeros_like(acc)
-
     def strip(slot, x0, nx, side, send_sem, recv_sem):
         rows = pl.ds(2 + HALO + x0, nx)
         src = pl.ds(HALO, HALO) if side == 0 else pl.ds(HALO + CZ - HALO, HALO)
@@ -156,6 +161,13 @@
         return strip(NCOMP + c, i * CHUNK, CHUNK, side, zt_send.at[k], zt_recv.at[k])
 
     loads(False)
+    near, far = DIFFUSE * 16.0 / 12.0, DIFFUSE / 12.0
+    push = TIME_STEP * vel_ref[...]
+    coef_ref[0:1, :] = push * (8.0 / 12.0) + near
+    coef_ref[1:2, :] = push * (-8.0 / 12.0) + near
+    coef_ref[2:3, :] = push * (-1.0 / 12.0) - far
+    coef_ref[3:4, :] = push * (1.0 / 12.0) - far
+    coef_ref[4:5, :] = -TIME_STEP * shear_ref[...]
     for c in range(NCOMP):
         for side in range(2):
             tan_strip(c, side).start()
@@ -199,8 +211,16 @@
             device_id=group_b[o], device_id_type=MESH)
 
     def outflow(c):
-        return pltpu.make_async_remote_copy(
-            src_ref=osend.at[c], dst_ref=orecv.at[c], send_sem=o_send.at[c], recv_sem=o_recv.at[c],
+        sides = pl.ds(1, 1) if c == 0 else pl.ds(0, 2)
+        return pltpu.make_async_remote_copy(
+            src_ref=osend.at[c, sides], dst_ref=orecv.at[c, sides],
+            send_sem=o_send.at[c], recv_sem=o_recv.at[c],
+            device_id=partner, device_id_type=MESH)
+
+    def raw_outflow(a):
+        return pltpu.make_async_remote_copy(
+            src_ref=res.at[a, 0, pl.ds(HALO + CX, HALO)], dst_ref=oraw.at[a],
+            send_sem=or_send.at[a], recv_sem=or_recv.at[a],
             device_id=partner, device_id_type=MESH)
 
     def reduce_all():
@@ -226,62 +246,76 @@
     def send_outflow(c):
         along = acc[0, 0:1, 0:1]
 
-        def put(i, _):
-            osend[c, 0, i] = res[1, c, HALO + CX + i] - along * res[0, c, HALO + CX + i]
-            osend[c, 1, i] = res[1, c, i] - along * res[0, c, i]
-            return 0
-
-        lax.fori_loop(0, HALO, put, 0)
+        for side, at in ((0, HALO + CX), (1, 0)):
+            if c > 0 or side > 0:
+                osend[c, side] = res[1, c, at:at + HALO] - along * res[0, c, at:at + HALO]
         outflow(c).start()
 
     bufs = (b0, w1, w2, w3)
 
-    def step(k, n, a, c):
+    def advance(k, n, a, c, first, count, sheared):
         half_set = jnp.minimum(c, 1)
         z = ZOUT[k]
+        m = count * z
         src = bufs[k]
         slot = n if k == 0 else half_set
         slot0 = a * NCOMP if k == 0 else 0
-        sheared = jnp.where(c == 1, 1.0, 0.0).astype(jnp.float32)
-
-        def block(b, _):
-            for p in range(XB // 2):
-                for h in range(2):
-                    cs = [coef_ref[r:r + 1, h * LANES:(h + 1) * LANES] for r in range(5)]
-                    shear = cs[4] * sheared
-                    both = []
-                    for q in range(2):
-                        i = b * XB + 2 * p + q
-
-                        def at(dx, dz):
-                            return src[slot, h, i + 2 + dx, 2 + dz:2 + dz + z, :]
-
-                        e = 0.5 * at(0, 0)
-                        e += (DIFFUSE * 16.0 / 12.0) * (at(0, 1) + at(0, -1))
-                        e += (-DIFFUSE / 12.0) * (at(0, 2) + at(0, -2))
-                        e += cs[0] * at(1, 0) + cs[1] * at(-1, 0)
-                        e += cs[2] * at(2, 0) + cs[3] * at(-2, 0)
-                        e += shear * src[slot0, h, i + 2, 2:2 + z, :]
-                        both.append(e)
-                    e = jnp.concatenate(both, axis=0)
-                    hi = e.astype(jnp.bfloat16)
-                    lo = (e - hi.astype(jnp.float32)).astype(jnp.bfloat16)
-                    ehi[2 * p * z:2 * (p + 1) * z, h * LANES:(h + 1) * LANES] = hi
-                    elo[2 * p * z:2 * (p + 1) * z, h * LANES:(h + 1) * LANES] = lo
-            m = XB * z
-            out = jnp.dot(ehi[:m], hhi_ref[...], preferred_element_type=jnp.float32)
-            out += jnp.dot(elo[:m], hhi_ref[...], preferred_element_type=jnp.float32)
-            out += jnp.dot(ehi[:m], hlo_ref[...], preferred_element_type=jnp.float32)
-            if k < 3:
-                dst = bufs[k + 1]
-                for h in range(2):
-                    dst[half_set, h, pl.ds(2 + b * XB, XB), 0:z, :] = out[
-                        :, h * LANES:(h + 1) * LANES].reshape(XB, z, LANES)
-            else:
-                res[a, c, pl.ds(b * XB, XB)] = out.reshape(XB, z, 2 * LANES)
-            return 0
-
-        lax.fori_loop(0, NXO // XB, block, 0)
+        for h in range(2):
+            cols = slice(h * LANES, (h + 1) * LANES)
+            cs = [coef_ref[r:r + 1, cols] for r in range(5)]
+            rows = {}
+
+            def row(i):
+                if i not in rows:
+                    rows[i] = src[slot, h, first + i, 2:2 + z, :]
+                return rows[i]
+
+            for p in range(count // 2):
+                both = []
+                for i in (2 * p, 2 * p + 1):
+
+                    def at(dz):
+                        return src[slot, h, first + i + 2, 2 + dz:2 + dz + z, :]
+
+                    e = 0.5 * row(i + 2)
+                    e += (DIFFUSE * 16.0 / 12.0) * (at(1) + at(-1))
+                    e += (-DIFFUSE / 12.0) * (at(2) + at(-2))
+                    e += cs[0] * row(i + 3) + cs[1] * row(i + 1)
+                    e += cs[2] * row(i + 4) + cs[3] * row(i)
+                    if sheared:
+                        e += cs[4] * src[slot0, h, first + i + 2, 2:2 + z, :]
+                    both.append(e)
+                e = jnp.concatenate(both, axis=0)
+                hi = e.astype(jnp.bfloat16)
+                ehi[2 * p * z:2 * (p + 1) * z, cols] = hi
+                elo[2 * p * z:2 * (p + 1) * z, cols] = (e - hi.astype(jnp.float32)).astype(jnp.bfloat16)
+        high = ehi[:m]
+        out = jnp.dot(
+            jnp.concatenate([high, elo[:m], high], axis=1),
+            jnp.concatenate([hhi_ref[...], hhi_ref[...], hlo_ref[...]], axis=0),
+            preferred_element_type=jnp.float32,
+        )
+        if k < 3:
+            for h in range(2):
+                bufs[k + 1][half_set, h, pl.ds(2 + first, count), 0:z, :] = out[
+                    :, h * LANES:(h + 1) * LANES].reshape(count, z, LANES)
+        else:
+            res[a, c, pl.ds(first, count)] = out.reshape(count, z, 2 * LANES)
+
+    def steps(n, a, c, sheared):
+        for k in range(4):
+            def block(b, _):
+                advance(k, n, a, c, b * XB, XB, sheared)
+                return 0
+
+            lax.fori_loop(0, NXO // XB, block, 0)
+            sent = n * 4 + k
+
+            @pl.when(sent < NCOMP * NCH - AHEAD)
+            def _():
+                t_copy(sent // NCH, lax.rem(sent, NCH)).wait_send()
+                later = sent + AHEAD
+                t_copy(later // NCH, lax.rem(later, NCH)).start()
 
     def item(n, _):
         a, c = n // NCOMP, lax.rem(n, NCOMP)
@@ -297,6 +331,8 @@
 
         @pl.when(n == 2 * NCOMP - 1)
         def _():
+            for d in range(2):
+                raw_outflow(d).start()
             reduce_all()
             for d in range(NCOMP - 1):
                 send_outflow(d)
@@ -310,13 +346,26 @@
 
             lax.fori_loop(0, NCH, strips, 0)
 
-        for k in range(4):
-            step(k, n, a, c)
+        @pl.when(n == 2 * NCOMP - 1)
+        def _():
+            for k in range(4):
+                def edge(e, _):
+                    advance(k, n, a, c, HALO - 2 * (k + 1) + e * (CX + 4 * (k + 1) - HALO), HALO, False)
+                    return 0
+
+                lax.fori_loop(0, 2, edge, 0)
+            send_outflow(NCOMP - 1)
+
+        @pl.when(c == 1)
+        def _():
+            steps(n, a, c, True)
+
+        @pl.when(c != 1)
+        def _():
+            steps(n, a, c, False)
         return 0
 
     lax.fori_loop(0, 2 * NCOMP, item, 0)
-    send_outflow(NCOMP - 1)
-
     along = acc[0, 0:1, 0:1]
 
     def write(c, lo, n, k):
@@ -326,21 +375,23 @@
     inner = CX - 2 * HALO
     for c in range(NCOMP):
         def mix(i, _):
-            tb[c, HALO + i] = res[1, c, 2 * HALO + i] - along * res[0, c, 2 * HALO + i]
+            rows = pl.ds(2 * HALO + i * HALO, HALO)
+            tb[c, pl.ds(HALO + i * HALO, HALO)] = res[1, c, rows] - along * res[0, c, rows]
             return 0
 
-        lax.fori_loop(0, inner, mix, 0)
+        lax.fori_loop(0, inner // HALO, mix, 0)
         write(c, HALO, inner, 0).start()
+    for d in range(2):
+        raw_outflow(d).wait_recv()
     for c in range(NCOMP):
         outflow(c).wait_recv()
-
-        def edges(i, _):
-            for side, at in ((0, 0), (1, CX - HALO)):
-                own = res[1, c, HALO + at + i] - along * res[0, c, HALO + at + i]
-                tb[c, at + i] = own + orecv[c, side, i]
-            return 0
-
-        lax.fori_loop(0, HALO, edges, 0)
+        for side, at in ((0, 0), (1, CX - HALO)):
+            own = res[1, c, HALO + at:2 * HALO + at] - along * res[0, c, HALO + at:2 * HALO + at]
+            if c == 0 and side == 0:
+                other = oraw[1] - along * oraw[0]
+            else:
+                other = orecv[c, side]
+            tb[c, at:at + HALO] = own + other
         write(c, 0, HALO, 1).start()
         write(c, CX - HALO, HALO, 2).start()
 
@@ -354,9 +405,14 @@
 
         @pl.loop(0, NCH)
         def _(i):
-            t_copy(c, i).wait_send()
+            @pl.when(c * NCH + i >= NCOMP * NCH - AHEAD)
+            def _():
+                t_copy(c, i).wait_send()
+
             start_strip(c, i, 0).wait_send()
             start_strip(c, i, 1).wait_send()
+    for d in range(2):
+        raw_outflow(d).wait_send()
     for o in range(3):
         reduce_a(o).wait_send()
     for o in range(nz - 1):
@@ -367,29 +423,16 @@
     table = wall_table(base_velocity.shape[0])
     high = table.astype(ml_dtypes.bfloat16)
     low = (table - high.astype(np.float32)).astype(ml_dtypes.bfloat16)
-    near, far = DIFFUSE * 16.0 / 12.0, DIFFUSE / 12.0
-    push = TIME_STEP * base_velocity
-    coefs = jnp.stack(
-        [
-            push * (8.0 / 12.0) + near,
-            push * (-8.0 / 12.0) + near,
-            push * (-1.0 / 12.0) - far,
-            push * (1.0 / 12.0) - far,
-            -TIME_STEP * base_shear,
-        ]
-        + [jnp.zeros_like(push)] * 3
-    )
     nz = sizes[2] // 2
     f32 = jnp.float32
     dma = pltpu.SemaphoreType.DMA
-    hbm = pl.BlockSpec(memory_space=pl.ANY)
-    vmem = pl.BlockSpec(memory_space=pltpu.VMEM)
+    hbm = pl.BlockSpec(memory_space=pltpu.HBM)
     lanes2 = 2 * LANES
     return pl.pallas_call(
         functools.partial(kernel, sizes),
         out_shape=jax.ShapeDtypeStruct(terminal.shape, f32),
-        in_specs=[hbm, hbm, hbm, vmem, vmem, vmem],
-        out_specs=hbm,
+        in_specs=[hbm] * 7,
+        out_specs=pl.BlockSpec(memory_space=pl.ANY),
         scratch_shapes=[
             pltpu.VMEM((NCOMP, CX, CZ, lanes2), f32),
             pltpu.VMEM((2 * NCOMP, 2, NXB, ZIN, LANES), f32),
@@ -399,14 +442,21 @@
             pltpu.VMEM((2, NCOMP, NXO, CZ, lanes2), f32),
             pltpu.VMEM((NCOMP, 2, HALO, CZ, lanes2), f32),
             pltpu.VMEM((NCOMP, 2, HALO, CZ, lanes2), f32),
+            pltpu.VMEM((2, HALO, CZ, lanes2), f32),
             pltpu.VMEM((XB * ZBUF, lanes2), jnp.bfloat16),
             pltpu.VMEM((XB * ZBUF, lanes2), jnp.bfloat16),
+            pltpu.VMEM((1, lanes2), f32),
+            pltpu.VMEM((1, lanes2), f32),
+            pltpu.VMEM((lanes2, lanes2), jnp.bfloat16),
+            pltpu.VMEM((lanes2, lanes2), jnp.bfloat16),
+            pltpu.VMEM((8, lanes2), f32),
             pltpu.VMEM((2, 8, LANES), f32),
             pltpu.VMEM((8, LANES), f32),
             pltpu.VMEM((3, 8, LANES), f32),
             pltpu.VMEM((8, LANES), f32),
             pltpu.VMEM((nz - 1, 8, LANES), f32),
             dma((4 * NCOMP,)),
+            dma((4,)),
             dma((NCOMP * NCH,)),
             dma((NCOMP * NCH,)),
             dma((NCOMP * 2,)),
@@ -419,12 +469,21 @@
             dma((nz - 1,)),
             dma((NCOMP,)),
             dma((NCOMP,)),
+            dma((2,)),
+            dma((2,)),
             dma((3 * NCOMP,)),
         ],
         compiler_params=pltpu.CompilerParams(
-            collective_id=0, has_side_effects=True, vmem_limit_bytes=58 * 1024 * 1024
+            collective_id=0, has_side_effects=True, vmem_limit_bytes=50 * 1024 * 1024
         ),
-    )(terminal, jump, tangent, coefs, jnp.asarray(high), jnp.asarray(low))
+    )(*(
+        pltpu.with_memory_space_constraint(value, pltpu.HBM)
+        for value in (
+            terminal, jump, tangent,
+            base_velocity.reshape(1, -1), base_shear.reshape(1, -1),
+            jnp.asarray(high), jnp.asarray(low),
+        )
+    ))
 
 
 def solution(mesh):

time: 125 us -> 118 us (0.944); the launches traced: 124 us -> 118 us
  local copies, waits for them, and re-layouts: 4.48 us -> 1.67 us
  other arithmetic: 1.36 us -> 0 us
    unnamed x1, local copies, waits for them, and re-layouts: 3.86 us -> 1.67 us
where the time goes in v2:
time: 118 us
  Pallas kernels  117 us (99%)
  local copies, waits for them, and re-layouts  1.67 us (1%)
    pallas_call x1, Pallas kernels, shards(): pl.pallas_call(functools.partial(kernel, sizes), out_shape=jax.ShapeDtype...  117 us

profile of v2, /device:TPU:22, one launch (start us, length us, event | category | flops | bytes accessed | tf_op | source)
XLA Modules:
  0.0 118.4 jit_solution(16735241763256425869)
XLA Ops:
  0.0 116.7 %shard_map.73 = f32[1,3,64,16,256]{4,3,2,1,0:T(8,128)S(1)} custom-call(f32[1,3,64,16,256]{4,3,2,1,0:T(8,128)} %t_hbm.1, f32[1,3,64,16,256]{4,3,2,1,0:T(8,128)} %j_hbm.1, f32[1,3,64,16,256]{4,3,2,1,0:T(8,128)} %tan_hbm.1, f32[1,256]{1,0:T(1,128)} %bitcast.2, f32[1,256]{1,0:T(1,128)} %bitcast.3, bf16[256,256]{1,0:T(8,128)(2,1)} %constant.4.clone.hhi_hbm, ...), custom_call_target="tpu_custom_call" | custom-call | tf_op jit(solution)/shard_map/pallas_call | solution.py:431
  116.7 1.7 %copy.9 = f32[1,3,64,16,256]{4,3,2,1,0:T(8,128)} copy(f32[1,3,64,16,256]{4,3,2,1,0:T(8,128)S(1)} %shard_map.73) | data formatting | bytes 6291456

commit v3 on v2

--- a/solution.py
+++ b/solution.py
@@ -30,6 +30,7 @@
 CHUNK = 8
 NCH = CX // CHUNK
 AHEAD = 5
+LAG = 2
 
 
 def invert_newton(matrix):
@@ -168,9 +169,8 @@
     coef_ref[2:3, :] = push * (-1.0 / 12.0) - far
     coef_ref[3:4, :] = push * (1.0 / 12.0) - far
     coef_ref[4:5, :] = -TIME_STEP * shear_ref[...]
-    for c in range(NCOMP):
-        for side in range(2):
-            tan_strip(c, side).start()
+    for side in range(2):
+        tan_strip(0, side).start()
 
     def dot_rows(first, second):
         prod = first * second
@@ -185,20 +185,17 @@
 
     lax.fori_loop(0, NCOMP * NCH, square, 0)
 
-    def arrive(c):
-        def piece(i, _):
-            t_copy(c, i).wait_recv()
-            rows = pl.ds(2 + HALO + i * CHUNK, CHUNK)
-            for h in range(2):
-                started = b0[NCOMP + c, h, rows, HALO:HALO + CZ, :] + tb[
-                    c, pl.ds(i * CHUNK, CHUNK), :, h * LANES:(h + 1) * LANES]
-                b0[NCOMP + c, h, rows, HALO:HALO + CZ, :] = started
-                acc[0] += dot_rows(started, b0[c, h, rows, HALO:HALO + CZ, :])
-            start_strip(c, i, 0).start()
-            start_strip(c, i, 1).start()
-            return 0
-
-        lax.fori_loop(0, NCH, piece, 0)
+    def piece(j):
+        c, i = j // NCH, lax.rem(j, NCH)
+        t_copy(c, i).wait_recv()
+        rows = pl.ds(2 + HALO + i * CHUNK, CHUNK)
+        for h in range(2):
+            started = b0[NCOMP + c, h, rows, HALO:HALO + CZ, :] + tb[
+                c, pl.ds(i * CHUNK, CHUNK), :, h * LANES:(h + 1) * LANES]
+            b0[NCOMP + c, h, rows, HALO:HALO + CZ, :] = started
+            acc[0] += dot_rows(started, b0[c, h, rows, HALO:HALO + CZ, :])
+        start_strip(c, i, 0).start()
+        start_strip(c, i, 1).start()
 
     def reduce_a(o):
         return pltpu.make_async_remote_copy(
@@ -313,10 +310,15 @@
 
             @pl.when(sent < NCOMP * NCH - AHEAD)
             def _():
-                t_copy(sent // NCH, lax.rem(sent, NCH)).wait_send()
                 later = sent + AHEAD
                 t_copy(later // NCH, lax.rem(later, NCH)).start()
 
+            early = (sent >= 16) & (sent < 16 + LAG)
+
+            @pl.when((sent >= LAG) & jnp.logical_not(early) & (n < 2 * NCOMP - 1))
+            def _():
+                piece(sent - LAG)
+
     def item(n, _):
         a, c = n // NCOMP, lax.rem(n, NCOMP)
 
@@ -325,12 +327,23 @@
             for side in range(2):
                 tan_strip(c, side).wait_recv()
 
-        @pl.when(a == 1)
-        def _():
-            arrive(c)
+        @pl.when(n < NCOMP - 1)
+        def _():
+            for side in range(2):
+                tan_strip(n + 1, side).start()
+
+        @pl.when(n == 2 * NCOMP - 2)
+        def _():
+            for j in range(NCH * 2 - LAG, NCH * 2):
+                piece(jnp.int32(j))
 
         @pl.when(n == 2 * NCOMP - 1)
         def _():
+            def last(j, _):
+                piece(j)
+                return 0
+
+            lax.fori_loop(20 - LAG, NCOMP * NCH, last, 0)
             for d in range(2):
                 raw_outflow(d).start()
             reduce_all()
@@ -405,10 +418,7 @@
 
         @pl.loop(0, NCH)
         def _(i):
-            @pl.when(c * NCH + i >= NCOMP * NCH - AHEAD)
-            def _():
-                t_copy(c, i).wait_send()
-
+            t_copy(c, i).wait_send()
             start_strip(c, i, 0).wait_send()
             start_strip(c, i, 1).wait_send()
     for d in range(2):

time: 118 us -> 109 us (0.924)
  Pallas kernels: 117 us -> 107 us
    pallas_call x1, Pallas kernels: 117 us -> 107 us  [shards(): pl.pallas_call(functools.partial(kernel, sizes), out_shape=jax.ShapeDtype...]
where the time goes in v3:
time: 109 us
  Pallas kernels  107 us (98%)
  local copies, waits for them, and re-layouts  1.67 us (2%)
    pallas_call x1, Pallas kernels, shards(): pl.pallas_call(functools.partial(kernel, sizes), out_shape=jax.ShapeDtype...  107 us

profile of v3, /device:TPU:22, one launch (start us, length us, event | category | flops | bytes accessed | tf_op | source)
XLA Modules:
  0.0 108.8 jit_solution(17513161624852337091)
XLA Ops:
  0.0 107.1 %shard_map.73 = f32[1,3,64,16,256]{4,3,2,1,0:T(8,128)S(1)} custom-call(f32[1,3,64,16,256]{4,3,2,1,0:T(8,128)} %t_hbm.1, f32[1,3,64,16,256]{4,3,2,1,0:T(8,128)} %j_hbm.1, f32[1,3,64,16,256]{4,3,2,1,0:T(8,128)} %tan_hbm.1, f32[1,256]{1,0:T(1,128)} %bitcast.2, f32[1,256]{1,0:T(1,128)} %bitcast.3, bf16[256,256]{1,0:T(8,128)(2,1)} %constant.4.clone.hhi_hbm, ...), custom_call_target="tpu_custom_call" | custom-call | tf_op jit(solution)/shard_map/pallas_call | solution.py:441
  107.1 1.7 %copy.9 = f32[1,3,64,16,256]{4,3,2,1,0:T(8,128)} copy(f32[1,3,64,16,256]{4,3,2,1,0:T(8,128)S(1)} %shard_map.73) | data formatting | bytes 6291456

commit v4 on v3

--- a/solution.py
+++ b/solution.py
@@ -29,8 +29,8 @@
 ZOUT = (32, 24, 24, 16)
 CHUNK = 8
 NCH = CX // CHUNK
-AHEAD = 5
-LAG = 2
+AHEAD = 7
+LAG = 3
 
 
 def invert_newton(matrix):
@@ -227,6 +227,8 @@
         ar_send[...] = jnp.where(row == 0, top, jnp.where(row == 1, low, 0.0))
         for o in range(3):
             reduce_a(o).start()
+        for d in range(2):
+            raw_outflow(d).start()
         for o in range(3):
             reduce_a(o).wait_recv()
         ar_mid[...] = ar_send[...] + ar_recv_a[0] + (ar_recv_a[1] + ar_recv_a[2])
@@ -344,8 +346,6 @@
                 return 0
 
             lax.fori_loop(20 - LAG, NCOMP * NCH, last, 0)
-            for d in range(2):
-                raw_outflow(d).start()
             reduce_all()
             for d in range(NCOMP - 1):
                 send_outflow(d)

time: 109 us -> 105 us (0.963)
  Pallas kernels: 107 us -> 104 us
    pallas_call x1, Pallas kernels: 107 us -> 104 us  [shards(): pl.pallas_call(functools.partial(kernel, sizes), out_shape=jax.ShapeDtype...]
where the time goes in v4:
time: 105 us
  Pallas kernels  104 us (99%)
  local copies, waits for them, and re-layouts  1.67 us (2%)
    pallas_call x1, Pallas kernels, shards(): pl.pallas_call(functools.partial(kernel, sizes), out_shape=jax.ShapeDtype...  104 us

profile of v4, /device:TPU:22, one launch (start us, length us, event | category | flops | bytes accessed | tf_op | source)
XLA Modules:
  0.0 105.2 jit_solution(13373013967562880928)
XLA Ops:
  0.0 103.5 %shard_map.73 = f32[1,3,64,16,256]{4,3,2,1,0:T(8,128)S(1)} custom-call(f32[1,3,64,16,256]{4,3,2,1,0:T(8,128)} %t_hbm.1, f32[1,3,64,16,256]{4,3,2,1,0:T(8,128)} %j_hbm.1, f32[1,3,64,16,256]{4,3,2,1,0:T(8,128)} %tan_hbm.1, f32[1,256]{1,0:T(1,128)} %bitcast.2, f32[1,256]{1,0:T(1,128)} %bitcast.3, bf16[256,256]{1,0:T(8,128)(2,1)} %constant.4.clone.hhi_hbm, ...), custom_call_target="tpu_custom_call" | custom-call | tf_op jit(solution)/shard_map/pallas_call | solution.py:441
  103.5 1.7 %copy.9 = f32[1,3,64,16,256]{4,3,2,1,0:T(8,128)} copy(f32[1,3,64,16,256]{4,3,2,1,0:T(8,128)S(1)} %shard_map.73) | data formatting | bytes 6291456

commit v5 on v4

--- a/solution.py
+++ b/solution.py
@@ -81,33 +81,33 @@
     group_b = [(seg, gx, lax.rem(zc + o, nz) * 2 + core) for o in range(1, nz)]
     outer = (seg, gx, lax.rem(gz + jnp.where(core == 0, ngz - 1, 1), ngz))
 
-    def loads(start):
-        for i, (src, dst) in enumerate((
-            (vel_hbm, vel_ref), (shear_hbm, shear_ref), (hhi_hbm, hhi_ref), (hlo_hbm, hlo_ref),
-        )):
-            cp = pltpu.make_async_copy(src, dst, const_sem.at[i])
-            if start:
-                cp.start()
-            else:
-                cp.wait()
-        for a, src in ((0, tan_hbm), (1, j_hbm)):
-            for c in range(NCOMP):
-                for h in range(2):
-                    cp = pltpu.make_async_copy(
-                        src.at[0, c, :, :, pl.ds(h * LANES, LANES)],
-                        b0.at[a * NCOMP + c, h, pl.ds(2 + HALO, CX), pl.ds(HALO, CZ), :],
-                        load_sem.at[(a * NCOMP + c) * 2 + h],
-                    )
-                    if start:
-                        cp.start()
-                    else:
-                        cp.wait()
+    def const_loads():
+        return [
+            pltpu.make_async_copy(src, dst, const_sem.at[i])
+            for i, (src, dst) in enumerate((
+                (vel_hbm, vel_ref), (shear_hbm, shear_ref), (hhi_hbm, hhi_ref), (hlo_hbm, hlo_ref),
+            ))
+        ]
+
+    def block_loads(a, c):
+        src = tan_hbm if a == 0 else j_hbm
+        return [
+            pltpu.make_async_copy(
+                src.at[0, c, :, :, pl.ds(h * LANES, LANES)],
+                b0.at[a * NCOMP + c, h, pl.ds(2 + HALO, CX), pl.ds(HALO, CZ), :],
+                load_sem.at[(a * NCOMP + c) * 2 + h],
+            )
+            for h in range(2)
+        ]
+
+    later_loads = [(0, 1), (0, 2), (1, 0), (1, 1), (1, 2)]
 
     barrier = pltpu.get_barrier_semaphore()
     peers = [(before, gx, gz), (after, gx, gz), outer] + group_a + group_b
     for d in peers:
         pl.semaphore_signal(barrier, inc=1, device_id=d, device_id_type=MESH)
-    loads(True)
+    for cp in block_loads(0, 0):
+        cp.start()
     pl.semaphore_wait(barrier, len(peers))
 
     def t_copy(c, i):
@@ -123,23 +123,12 @@
 
     for i in range(AHEAD):
         t_copy(i // NCH, i % NCH).start()
-
-    def zero_pads(s, _):
-        for h in range(2):
-            for lo, hi in ((0, 2 + HALO), (2 + HALO + CX, NXB)):
-                b0[s, h, lo:hi, :, :] = jnp.zeros((hi - lo, ZIN, LANES), jnp.float32)
-            b0[s, h, 2 + HALO:2 + HALO + CX, 2 * HALO + CZ:, :] = jnp.zeros(
-                (CX, ZIN - 2 * HALO - CZ, LANES), jnp.float32)
-        return 0
-
-    lax.fori_loop(0, 2 * NCOMP, zero_pads, 0)
-    for w in (w1, w2, w3):
-        for s in range(2):
-            for h in range(2):
-                for lo in (0, NXB - 2):
-                    w[s, h, lo:lo + 2, :, :] = jnp.zeros((2, ZBUF, LANES), jnp.float32)
-                w[s, h, 2:NXB - 2, 24:, :] = jnp.zeros((NXB - 4, 8, LANES), jnp.float32)
-    acc[...] = jnp.zeros_like(acc)
+    for cp in const_loads():
+        cp.start()
+    for which in later_loads:
+        for cp in block_loads(*which):
+            cp.start()
+
     def strip(slot, x0, nx, side, send_sem, recv_sem):
         rows = pl.ds(2 + HALO + x0, nx)
         src = pl.ds(HALO, HALO) if side == 0 else pl.ds(HALO + CZ - HALO, HALO)
@@ -161,7 +150,32 @@
         k = (c * NCH + i) * 2 + side
         return strip(NCOMP + c, i * CHUNK, CHUNK, side, zt_send.at[k], zt_recv.at[k])
 
-    loads(False)
+    for cp in block_loads(0, 0):
+        cp.wait()
+    for side in range(2):
+        tan_strip(0, side).start()
+
+    def zero_pads(s, _):
+        for h in range(2):
+            for lo, hi in ((0, 2 + HALO), (2 + HALO + CX, NXB)):
+                b0[s, h, lo:hi, :, :] = jnp.zeros((hi - lo, ZIN, LANES), jnp.float32)
+            b0[s, h, 2 + HALO:2 + HALO + CX, 2 * HALO + CZ:, :] = jnp.zeros(
+                (CX, ZIN - 2 * HALO - CZ, LANES), jnp.float32)
+        return 0
+
+    lax.fori_loop(0, 2 * NCOMP, zero_pads, 0)
+    for w in (w1, w2, w3):
+        for s in range(2):
+            for h in range(2):
+                for lo in (0, NXB - 2):
+                    w[s, h, lo:lo + 2, :, :] = jnp.zeros((2, ZBUF, LANES), jnp.float32)
+                w[s, h, 2:NXB - 2, 24:, :] = jnp.zeros((NXB - 4, 8, LANES), jnp.float32)
+    acc[...] = jnp.zeros_like(acc)
+    for cp in const_loads():
+        cp.wait()
+    for which in later_loads:
+        for cp in block_loads(*which):
+            cp.wait()
     near, far = DIFFUSE * 16.0 / 12.0, DIFFUSE / 12.0
     push = TIME_STEP * vel_ref[...]
     coef_ref[0:1, :] = push * (8.0 / 12.0) + near
@@ -169,8 +183,6 @@
     coef_ref[2:3, :] = push * (-1.0 / 12.0) - far
     coef_ref[3:4, :] = push * (1.0 / 12.0) - far
     coef_ref[4:5, :] = -TIME_STEP * shear_ref[...]
-    for side in range(2):
-        tan_strip(0, side).start()
 
     def dot_rows(first, second):
         prod = first * second

time: 105 us -> 105 us (level)
  no operation moved by 1% of the time
where the time goes in v5:
time: 105 us
  Pallas kernels  103 us (98%)
  local copies, waits for them, and re-layouts  1.67 us (2%)
    pallas_call x1, Pallas kernels, shards(): pl.pallas_call(functools.partial(kernel, sizes), out_shape=jax.ShapeDtype...  103 us

profile of v5, /device:TPU:22, one launch (start us, length us, event | category | flops | bytes accessed | tf_op | source)
XLA Modules:
  0.0 105.0 jit_solution(15210583475808627167)
XLA Ops:
  0.0 103.3 %shard_map.73 = f32[1,3,64,16,256]{4,3,2,1,0:T(8,128)S(1)} custom-call(f32[1,3,64,16,256]{4,3,2,1,0:T(8,128)} %t_hbm.1, f32[1,3,64,16,256]{4,3,2,1,0:T(8,128)} %j_hbm.1, f32[1,3,64,16,256]{4,3,2,1,0:T(8,128)} %tan_hbm.1, f32[1,256]{1,0:T(1,128)} %bitcast.2, f32[1,256]{1,0:T(1,128)} %bitcast.3, bf16[256,256]{1,0:T(8,128)(2,1)} %constant.4.clone.hhi_hbm, ...), custom_call_target="tpu_custom_call" | custom-call | tf_op jit(solution)/shard_map/pallas_call | solution.py:453
  103.3 1.7 %copy.9 = f32[1,3,64,16,256]{4,3,2,1,0:T(8,128)} copy(f32[1,3,64,16,256]{4,3,2,1,0:T(8,128)S(1)} %shard_map.73) | data formatting | bytes 6291456
